TPU v7x, 32 devices: a whole 2x2x4 slice. The times are simulated.
32 devices in a mesh: row: 4 (over y, x), col: 8 (over z, core).
Axes of the slice: x: 2, y: 2, z: 4, core: 2. Of those that a mesh axis runs over, the one named last changes fastest.
Arguments:
- vectors: bfloat16 [512, 8192], P('row', 'col'), may hold values from -6 to 6
- factor_tiles: bfloat16 [32, 24, 256, 256], P('row', 'col'), may hold values from -0.109375 to 0.109375
- tile_columns: int32 [32, 24], P('row', 'col'), may hold values from 0 to 31, as said below
- live_counts: int32 [32, 8], P('row', 'col'), may hold values from 0 to 3, as said below
Outputs:
- applied: float32 [512, 8192], P('row', 'col')
Inputs may be any that keep to these rules, and one draw needn't show every extreme that they name: `tile_columns`: slot s holds a tile column in [(s // 3) * 4, (s // 3 + 1) * 4); the slots of one row tile name distinct columns; a live slot's column is at most its row tile; the row tile's own column is always live, in the first slot of its group. `live_counts`: counts never exceed the columns allowed in that group, so the upper right region of groups is empty. In group 0 every row tile i >= 2 has exactly 3 live slots.
All inputs are finite; a program needn't handle non-finite values.
Results may differ from a plain program's by a relative error of at most 0.002.
Values may be sent and summed in bfloat16 or wider, within the bound.
A program may use at most 64 MiB of HBM per device.

v0:
```python
import jax
import jax.numpy as jnp
from jax import lax
from jax.sharding import PartitionSpec as P


def per_device(vectors, factor_tiles, tile_columns, live_counts):
    row_tiles = factor_tiles.shape[0]
    slot_count = factor_tiles.shape[1]
    tile_size = factor_tiles.shape[2]
    col_tiles = vectors.shape[1] // tile_size
    offset = lax.axis_index("col") * col_tiles
    local_cols = tile_columns - offset
    slot_index = lax.broadcasted_iota(jnp.int32, (row_tiles, slot_count), 1)
    live_mask = (slot_index < live_counts).astype(jnp.float32)
    column_iota = lax.broadcasted_iota(jnp.int32, (row_tiles, slot_count, col_tiles), 2)
    select_map = (local_cols[:, :, None] == column_iota).astype(jnp.float32) * live_mask[:, :, None]
    select_half = select_map.astype(jnp.bfloat16)
    vector_rows = lax.all_gather(vectors, "row", axis=0, tiled=True)
    count_rows = vector_rows.shape[0]
    blocks = vector_rows.reshape(count_rows, col_tiles, tile_size)
    picked = jnp.einsum(
        "tkj,vjc->tkvc", select_half, blocks, preferred_element_type=jnp.float32
    ).astype(jnp.bfloat16)
    partial_value = jnp.einsum(
        "tkab,tkvb->vta", factor_tiles, picked, preferred_element_type=jnp.float32
    )
    partial_all = partial_value.reshape(count_rows, row_tiles * tile_size)
    rowvals = lax.psum(partial_all, "col").astype(jnp.bfloat16)
    count_rows = rowvals.shape[0]
    weights = rowvals.reshape(count_rows, row_tiles, tile_size)
    contrib = jnp.einsum(
        "tkab,vta->tkvb", factor_tiles, weights, preferred_element_type=jnp.float32
    )
    summed = jnp.einsum("tkj,tkvb->vjb", select_map, contrib, precision=lax.Precision.HIGHEST)
    return lax.psum_scatter(
        summed.reshape(count_rows, col_tiles * tile_size), "row", scatter_dimension=0, tiled=True
    )


def solution(mesh):
    in_specs = (P("row", "col"), P("row", "col", None, None), P("row", "col"), P("row", "col"))
    out_specs = P("row", "col")
    return jax.shard_map(
        per_device, mesh=mesh, in_specs=in_specs, out_specs=out_specs, check_vma=False
    )
```

profile of v0, /device:TPU:0, one launch (start us, length us, event | category | flops | bytes accessed | tf_op | source)
XLA Modules:
  0.0 195.0 jit_solution(5123145907293766464)
XLA Ops:
  6.5 0.0 copy-start
  6.5 0.0 all-gather.2.cloned.1.call-start
  6.5 0.7 all-gather.2.cloned.1.call-update
  7.3 0.0 reduce-scatter.2.cloned.1.call-start
  7.3 0.8 fusion.13
  8.1 0.7 broadcast_subtract_fusion
  8.8 29.6 %all-gather.2.cloned.1.call-done = bf16[512,1024]{1,0:T(8,128)(2,1)} async-done(((bf16[128,1024]{1,0:T(8,128)(2,1)}), bf16[512,1024]{1,0:T(8,128)(2,1)}) %all-gather.2.cloned.1.call-update) | async-done | bytes 1048592 | tf_op jit(solution)/shard_map/all_gather | solution.py:19
  38.4 2.6 %reshape.39 = bf16[512,4,256,1]{2,1,0,3:T(4,128)(2,1)} reshape(bf16[512,1024]{1,0:T(8,128)(2,1)} %all-gather.2.cloned.1.call-done) | data formatting | bytes 2097152 | tf_op jit(solution)/shard_map/reshape | solution.py:21
  41.1 3.5 %fusion.5 = bf16[8,3,512,256]{3,0,2,1:T(8,128)(2,1)S(1)} fusion(bf16[512,4,256,1]{2,1,0,3:T(4,128)(2,1)} %reshape.39, f32[8,3]{0,1:T(4,128)S(1)} %fusion.13, s32[8,3]{0,1:T(4,128)S(1)} %broadcast_subtract_fusion), kind=kOutput, calls=%fused_computation.9 | convolution fusion | flops 25166016 | bytes 7340224 | tf_op jit(solution)/shard_map/tkj,vjc->tkvc/dot_general | solution.py:22
  44.6 0.0 copy-done
  44.6 4.1 %fusion.3 = f32[8,512,256,1]{1,2,3,0:T(8,128)} fusion(bf16[8,3,256,256]{3,2,1,0:T(8,128)(2,1)S(1)} %copy-done, bf16[8,3,512,256]{3,0,2,1:T(8,128)(2,1)S(1)} %fusion.5), kind=kOutput, calls=%fused_computation.4 | convolution fusion | flops 1610612736 | bytes 13631488 | tf_op jit(solution)/shard_map/tkab,tkvb->vta/dot_general | solution.py:25
  48.7 89.4 %all-reduce.1 = bf16[512,2048]{0,1:T(8,128)(2,1)} all-reduce(f32[512,2048]{0,1:T(8,128)} %bitcast.33), channel_id=1, replica_groups=mesh['row'=4,'col'=8] {'col'}, use_global_device_ids=true, to_apply=%region_0.0 | all-reduce | flops 1048576 | bytes 6291456 | tf_op jit(solution)/shard_map/psum | solution.py:29
  138.1 3.4 %fusion.16 = f32[8,512,3,256]{3,1,2,0:T(8,128)S(1)} fusion(bf16[512,8,256,1]{0,2,3,1:T(8,128)(2,1)} %bitcast.34, bf16[8,3,256,256]{3,2,1,0:T(8,128)(2,1)S(1)} %copy-done), kind=kOutput, calls=%fused_computation.21 | convolution fusion | flops 1610612736 | bytes 17825792 | tf_op jit(solution)/shard_map/tkab,vta->tkvb/dot_general | solution.py:32
  141.5 11.5 %fusion = f32[512,256,4,1]{1,2,3,0:T(4,128)S(1)} fusion(f32[8,512,3,256]{3,1,2,0:T(8,128)S(1)} %fusion.16, f32[8,3]{0,1:T(4,128)S(1)} %fusion.13, s32[8,3]{0,1:T(4,128)S(1)} %broadcast_subtract_fusion), kind=kOutput, calls=%fused_computation | convolution fusion | flops 150995136 | bytes 14680256 | tf_op jit(solution)/shard_map/tkj,tkvb->vjb/dot_general | solution.py:35
  153.0 1.8 copy.11
  154.8 0.0 reduce-scatter.2.cloned.1.call-update
  154.9 33.3 %reduce-scatter.2.cloned.1.call-done = f32[128,1024]{1,0:T(8,128)} async-done(((f32[512,1024]{1,0:T(8,128)}), f32[128,1024]{1,0:T(8,128)}) %reduce-scatter.2.cloned.1.call-update) | async-done | bytes 524304 | tf_op jit(solution)/shard_map/reduce_scatter | solution.py:36
Async XLA Ops:
  6.5 38.1 %copy-start = (bf16[8,3,256,256]{3,2,1,0:T(8,128)(2,1)S(1)}, bf16[8,3,256,256]{3,2,1,0:T(8,128)(2,1)}, u32[]{:S(2)}) copy-start(bf16[8,3,256,256]{3,2,1,0:T(8,128)(2,1)} %param.5) | copy-start | bytes 9437188
  6.5 31.9 %all-gather.2.cloned.1.call-start = ((), (), s32[]{:S(2)}) async-start(), calls=%async_computation.1 | async-start | bytes 1310720 | tf_op jit(solution)/shard_map/all_gather | solution.py:19
  7.3 180.9 %reduce-scatter.2.cloned.1.call-start = ((), (), s32[]{:S(2)}) async-start(), calls=%async_computation.2 | async-start | bytes 2621440 | tf_op jit(solution)/shard_map/reduce_scatter | solution.py:36
Sparse Core Ops, SparseCore 0:
  9.2 29.2 all-gather.1
  155.0 33.1 reduce-scatter.1
where the time goes:
time: 195 us
  blocking collectives  89.4 us (46%)
  waiting for transfers between devices  63.7 us (33%)
  matrix products  22.5 us (12%)
  between operations  13.4 us (7%)
  local copies, waits for them, and re-layouts  4.45 us (2%)
    psum x1, blocking collectives, per_device(): rowvals = lax.psum(partial_all, 'col').astype(jnp.bfloat16)  89.4 us
    reduce_scatter x1, waiting for transfers between devices, per_device(): lax.psum_scatter(summed.reshape(count_rows, col_tiles * tile_size), 'row'...  33.3 us
    all_gather x1, waiting for transfers between devices, per_device(): vector_rows = lax.all_gather(vectors, 'row', axis=0, tiled=True)  29.6 us
    dot_general x1, matrix products, per_device(): jnp.einsum('tkj,tkvb->vjb', select_map, contrib, precision=lax.Precision....  11.5 us
    dot_general x1, matrix products, per_device(): jnp.einsum('tkab,tkvb->vta', factor_tiles, picked, preferred_element_type...  4.12 us
  transfers between devices with their start and end apart: 2, of which 2 were waited for; matrix products, arithmetic and copies ran while one was open for 1% of the time, Pallas kernels for 0%

commit v1 on v0

v1 whole, which is shorter than its diff:
```python
import functools

import jax
import jax.numpy as jnp
from jax import lax
from jax.experimental import pallas as pl
from jax.experimental.pallas import tpu as pltpu
from jax.sharding import PartitionSpec as P

LANES = 128
GROUP = 16
PEAK = 32000.0
MESH = pl.DeviceIdType.MESH


def xor(a, b, size):
    both, bit = 0, 1
    while bit < size:
        both = both + bit * ((a // bit) % 2) * ((b // bit) % 2)
        bit *= 2
    return a + b - 2 * both


def encode(value, ref):
    rows, width = value.shape
    most = jnp.full((GROUP, LANES), 1e-30, jnp.float32)
    for at in range(width // LANES):
        part = jnp.abs(value[:, at * LANES:(at + 1) * LANES])
        most = jnp.maximum(most, jnp.max(part.reshape(rows // GROUP, GROUP, LANES), axis=0))
    power = jnp.ceil(jnp.log2(most))
    scale = jnp.tile(jnp.exp2(-power) * PEAK, (rows // GROUP, 1))
    for at in range(width // LANES):
        coded = jnp.round(value[:, at * LANES:(at + 1) * LANES] * scale)
        ref[at * rows:(at + 1) * rows, :] = coded.astype(jnp.int32).astype(jnp.int16)
    ref[rows * width // LANES:, :] = power.astype(jnp.int32).astype(jnp.int16)


def decode(ref, rows, width):
    power = ref[rows * width // LANES:, :].astype(jnp.int32).astype(jnp.float32)
    scale = jnp.tile(jnp.exp2(power) * (1.0 / PEAK), (rows // GROUP, 1))
    parts = [
        ref[at * rows:(at + 1) * rows, :].astype(jnp.int32).astype(jnp.float32) * scale
        for at in range(width // LANES)
    ]
    return jnp.concatenate(parts, axis=1)


def kernel(
    dims, cols_ref, counts_ref, v_hbm, f_hbm, out_ref,
    v_all, f_all, dense, own, pair_out, pair_in, held, chain_out, chain_in, cross_in, rowvals, part_out, part_in,
    load_sem, v_send, v_recv, pair_send, pair_recv, chain_send, chain_recv, cross_recv,
    far_send, far_recv, near_send, near_recv, part_send, part_recv,
):
    n_row, n_col, n_tiles, n_slots, tile, col_tiles, subs = dims
    n_pair = n_col // 2
    n_vec, width = out_ref.shape
    pieces, rows = n_row * subs, n_vec // subs
    half = n_tiles // 2 * tile

    me_row, me_col = lax.axis_index("row"), lax.axis_index("col")
    pair, core = me_col // 2, me_col % 2
    partner = pair * 2 + 1 - core

    def last_pair(row):
        return jnp.minimum(n_pair - 1, ((row + 1) * n_tiles - 1) // (2 * col_tiles))

    last = last_pair(me_row)
    middle = last // 2
    left = pair <= middle
    active = pair <= last
    solo = last == 0
    center = jnp.logical_and(jnp.logical_or(pair == middle, pair == middle + 1), last > 0)
    depth = jnp.where(left, pair, last - pair)
    spread = jnp.where(left, middle - pair, pair - middle - 1)
    has_outer = depth > 0
    outer = jnp.where(left, pair - 1, pair + 1)
    inner = jnp.where(left, pair + 1, pair - 1)
    outer_col, inner_col = outer * 2 + core, inner * 2 + core
    meet = jnp.where(solo, 0, 1 + jnp.maximum(middle, last - middle - 1))
    total_lag = meet + 1 + spread
    final_lag = total_lag + 1

    load_v = pltpu.make_async_copy(v_hbm, v_all.at[0], load_sem.at[0])
    load_f = pltpu.make_async_copy(f_hbm, f_all, load_sem.at[1])
    load_v.start()
    load_f.start()

    barrier = pltpu.get_barrier_semaphore()
    for k in range(1, n_row):
        pl.semaphore_signal(barrier, inc=1, device_id=(xor(me_row, k, n_row), me_col), device_id_type=MESH)
    pl.semaphore_signal(barrier, inc=1, device_id=(me_row, partner), device_id_type=MESH)

    @pl.when(pair > 0)
    def _():
        pl.semaphore_signal(barrier, inc=1, device_id=(me_row, me_col - 2), device_id_type=MESH)

    @pl.when(pair < n_pair - 1)
    def _():
        pl.semaphore_signal(barrier, inc=1, device_id=(me_row, me_col + 2), device_id_type=MESH)

    edges = jnp.where(pair > 0, 1, 0) + jnp.where(pair < n_pair - 1, 1, 0)
    pl.semaphore_wait(barrier, n_row + edges)

    def remote(src, dst, send, recv, row, col):
        return pltpu.make_async_remote_copy(
            src_ref=src, dst_ref=dst, send_sem=send, recv_sem=recv, device_id=(row, col), device_id_type=MESH
        )

    def v_copy(k):
        return remote(v_hbm, v_all.at[k], v_send.at[k], v_recv.at[k], xor(me_row, k, n_row), me_col)

    def pair_copy(j):
        return remote(pair_out.at[j], pair_in.at[j], pair_send.at[j], pair_recv.at[j], me_row, partner)

    def chain_copy(j):
        return remote(chain_out.at[j], chain_in.at[j], chain_send.at[j], chain_recv.at[j], me_row, inner_col)

    def cross_copy(j):
        return remote(chain_out.at[j], cross_in.at[j], chain_send.at[j], cross_recv.at[j], me_row, inner_col)

    def far_copy(j):
        return remote(rowvals.at[core, j], rowvals.at[core, j], far_send.at[j], far_recv.at[j], me_row, outer_col)

    def near_copy(j):
        return remote(rowvals.at[core, j], rowvals.at[core, j], near_send.at[j], near_recv.at[j], me_row, partner)

    def part_copy(j):
        return remote(
            part_out.at[j], part_in.at[j], part_send.at[j], part_recv.at[j], xor(me_row, j // subs, n_row), me_col
        )

    for k in range(1, n_row):
        @pl.when(pair <= last_pair(xor(me_row, k, n_row)))
        def _():
            v_copy(k).start()

    load_v.wait()
    load_f.wait()

    @pl.when(active)
    def _():
        @pl.loop(0, n_tiles)
        def _(t):
            at = (t % (n_tiles // 2)) * tile
            zero = jnp.zeros((tile, tile), jnp.bfloat16)
            for c in range(col_tiles):
                value = zero
                for s in range(n_slots):
                    pick = jnp.logical_and(cols_ref[t, s] == me_col * col_tiles + c, s < counts_ref[t, 0])
                    value = jnp.where(pick, f_all[t, s], value)
                dense[t // (n_tiles // 2), pl.ds(pl.multiple_of(at, tile), tile), c * tile:(c + 1) * tile] = value

        @pl.loop(0, pieces + final_lag)
        def _(t):
            def valid(j):
                return jnp.logical_and(j >= 0, j < pieces)

            j_total = t - total_lag
            j_in = t - 1 - depth
            j_out = t - final_lag

            @pl.when(jnp.logical_and(valid(j_total), jnp.logical_not(solo)))
            def _():
                @pl.when(center)
                def _():
                    cross_copy(j_total).wait_recv()
                    total = held[j_total] + decode(cross_in.at[j_total], rows, half)
                    rowvals[core, j_total] = total.astype(jnp.bfloat16)

                @pl.when(jnp.logical_not(center))
                def _():
                    far_copy(j_total).wait_recv()

                @pl.when(has_outer)
                def _():
                    far_copy(j_total).start()

                near_copy(j_total).start()

            @pl.when(valid(j_in))
            def _():
                pair_copy(j_in).wait_recv()
                held[j_in] = own[j_in] + pair_in[j_in]

                @pl.when(has_outer)
                def _():
                    chain_copy(j_in).wait_recv()
                    held[j_in] += decode(chain_in.at[j_in], rows, half)

                @pl.when(solo)
                def _():
                    rowvals[core, j_in] = held[j_in].astype(jnp.bfloat16)
                    near_copy(j_in).start()

                @pl.when(jnp.logical_not(solo))
                def _():
                    encode(held[j_in], chain_out.at[j_in])

                    @pl.when(center)
                    def _():
                        cross_copy(j_in).start()

                    @pl.when(jnp.logical_not(center))
                    def _():
                        chain_copy(j_in).start()

            @pl.when(t < pieces)
            def _():
                k, sub = t // subs, t % subs

                @pl.when(jnp.logical_and(k > 0, sub == 0))
                def _():
                    v_copy(k).wait_recv()

                vec = v_all[k, pl.ds(pl.multiple_of(sub * rows, rows), rows), :]
                dims_nt = (((1,), (1,)), ((), ()))
                pair_out[t] = lax.dot_general(vec, dense[1 - core], dims_nt, preferred_element_type=jnp.float32)
                pair_copy(t).start()
                own[t] = lax.dot_general(vec, dense[core], dims_nt, preferred_element_type=jnp.float32)

            @pl.when(valid(j_out))
            def _():
                near_copy(j_out).wait_recv()
                part = jnp.dot(rowvals[0, j_out], dense[0], preferred_element_type=jnp.float32)
                part += jnp.dot(rowvals[1, j_out], dense[1], preferred_element_type=jnp.float32)

                @pl.when(j_out < subs)
                def _():
                    out_ref[pl.ds(pl.multiple_of(j_out * rows, rows), rows), :] = part

                @pl.when(j_out >= subs)
                def _():
                    encode(part, part_out.at[j_out])
                    part_copy(j_out).start()

    @pl.when(jnp.logical_not(active))
    def _():
        out_ref[...] = jnp.zeros_like(out_ref)

    @pl.loop(subs, pieces)
    def _(j):
        @pl.when(pair <= last_pair(xor(me_row, j // subs, n_row)))
        def _():
            part_copy(j).wait_recv()
            where = pl.ds(pl.multiple_of((j % subs) * rows, rows), rows)
            out_ref[where, :] += decode(part_in.at[j], rows, width)

    for k in range(1, n_row):
        @pl.when(pair <= last_pair(xor(me_row, k, n_row)))
        def _():
            v_copy(k).wait_send()

    @pl.when(active)
    def _():
        @pl.loop(0, pieces)
        def _(j):
            pair_copy(j).wait_send()
            near_copy(j).wait_send()

            @pl.when(jnp.logical_not(solo))
            def _():
                chain_copy(j).wait_send()

            @pl.when(has_outer)
            def _():
                far_copy(j).wait_send()

            @pl.when(j >= subs)
            def _():
                part_copy(j).wait_send()


def per_device(n_row, n_col, vectors, factor_tiles, tile_columns, live_counts):
    n_tiles, n_slots, tile, _ = factor_tiles.shape
    n_vec, width = vectors.shape
    subs = max(1, n_vec // 64)
    pieces, rows = n_row * subs, n_vec // subs
    half = n_tiles // 2 * tile
    coded = rows * half // LANES + GROUP
    coded_out = rows * width // LANES + GROUP
    dma = pltpu.SemaphoreType.DMA
    return pl.pallas_call(
        functools.partial(kernel, (n_row, n_col, n_tiles, n_slots, tile, width // tile, subs)),
        out_shape=jax.ShapeDtypeStruct((n_vec, width), jnp.float32),
        in_specs=[
            pl.BlockSpec(memory_space=pltpu.SMEM),
            pl.BlockSpec(memory_space=pltpu.SMEM),
            pl.BlockSpec(memory_space=pl.ANY),
            pl.BlockSpec(memory_space=pl.ANY),
        ],
        out_specs=pl.BlockSpec(memory_space=pltpu.VMEM),
        scratch_shapes=[
            pltpu.VMEM((n_row, n_vec, width), jnp.bfloat16),
            pltpu.VMEM((n_tiles, n_slots, tile, tile), jnp.bfloat16),
            pltpu.VMEM((2, half, width), jnp.bfloat16),
            pltpu.VMEM((pieces, rows, half), jnp.float32),
            pltpu.VMEM((pieces, rows, half), jnp.float32),
            pltpu.VMEM((pieces, rows, half), jnp.float32),
            pltpu.VMEM((pieces, rows, half), jnp.float32),
            pltpu.VMEM((pieces, coded, LANES), jnp.int16),
            pltpu.VMEM((pieces, coded, LANES), jnp.int16),
            pltpu.VMEM((pieces, coded, LANES), jnp.int16),
            pltpu.VMEM((2, pieces, rows, half), jnp.bfloat16),
            pltpu.VMEM((pieces, coded_out, LANES), jnp.int16),
            pltpu.VMEM((pieces, coded_out, LANES), jnp.int16),
            dma((2,)),
            dma((n_row,)), dma((n_row,)),
            dma((pieces,)), dma((pieces,)),
            dma((pieces,)), dma((pieces,)), dma((pieces,)),
            dma((pieces,)), dma((pieces,)),
            dma((pieces,)), dma((pieces,)),
            dma((pieces,)), dma((pieces,)),
        ],
        compiler_params=pltpu.CompilerParams(
            collective_id=0, has_side_effects=True, vmem_limit_bytes=56 * 1024 * 1024
        ),
    )(tile_columns, live_counts, vectors, factor_tiles)


def solution(mesh):
    in_specs = (P("row", "col"), P("row", "col", None, None), P("row", "col"), P("row", "col"))
    out_specs = P("row", "col")
    body = functools.partial(per_device, mesh.shape["row"], mesh.shape["col"])
    return jax.shard_map(body, mesh=mesh, in_specs=in_specs, out_specs=out_specs, check_vma=False)
```

time: 195 us -> 71.8 us (0.37)
  blocking collectives: 89.4 us -> 0 us
  Pallas kernels: 0 us -> 67 us
  waiting for transfers between devices: 63.7 us -> 0 us
  matrix products: 22.5 us -> 0 us
  between operations: 13.4 us -> 0.01 us
    psum x1 -> x0, blocking collectives: 89.4 us -> none  [per_device(): rowvals = lax.psum(partial_all, 'col').astype(jnp.bfloat16)]
    pallas_call x0 -> x1, Pallas kernels: none -> 67 us  [per_device(): pl.pallas_call(functools.partial(kernel, (n_row, n_col, n_tiles, n_slots,...]
    reduce_scatter x1 -> x0, waiting for transfers between devices: 33.3 us -> none  [per_device(): lax.psum_scatter(summed.reshape(count_rows, col_tiles * tile_size), 'row'...]
    all_gather x1 -> x0, waiting for transfers between devices: 29.6 us -> none  [per_device(): vector_rows = lax.all_gather(vectors, 'row', axis=0, tiled=True)]
    dot_general x4 -> x0, matrix products: 22.5 us -> none  [the longest x1 11.5 us: per_device(): jnp.einsum('tkj,tkvb->vjb', select_map, contrib, precision=lax.Precision....]
    unnamed x3, local copies, waits for them, and re-layouts: 1.81 us -> 4.55 us
    reshape x1 -> x0, local copies, waits for them, and re-layouts: 2.64 us -> none  [per_device(): blocks = vector_rows.reshape(count_rows, col_tiles, tile_size)]
  transfers between devices with their start and end apart: 2 -> 0, of which waited for: 2 -> 0; matrix products, arithmetic and copies ran while one was open for 1% -> 0% of each run, Pallas kernels for 0% -> 0%
where the time goes in v1:
time: 71.8 us; the launch traced here: 71.5 us
  Pallas kernels  67 us (93%)
  local copies, waits for them, and re-layouts  4.55 us (6%)
    pallas_call x1, Pallas kernels, per_device(): pl.pallas_call(functools.partial(kernel, (n_row, n_col, n_tiles, n_slots,...  67 us
    unnamed x3, local copies, waits for them, and re-layouts  4.55 us

profile of v1, /device:TPU:0, one launch (start us, length us, event | category | flops | bytes accessed | tf_op | source)
XLA Modules:
  0.0 71.5 jit_solution(16763936110208398575)
XLA Ops:
  0.0 1.3 %copy.5.cols_ref = s32[8,3]{1,0:T(8,128)} copy(s32[8,3]{0,1:T(4,128)} %param.6) | data formatting | bytes 192 | tf_op args[2]
  1.3 1.3 %copy.6.counts_ref = s32[8,1]{1,0:T(8,128)} copy(s32[8,1]{0,1:T(1,128)} %param.7) | data formatting | bytes 64 | tf_op args[3]
  2.7 67.0 %shard_map.46 = f32[128,1024]{1,0:T(8,128)} custom-call(s32[8,3]{1,0:T(8,128)} %copy.5.cols_ref, s32[8,1]{1,0:T(8,128)} %copy.6.counts_ref, bf16[128,1024]{1,0:T(8,128)(2,1)} %v_hbm.1, bf16[8,3,256,256]{3,2,1,0:T(8,128)(2,1)} %f_hbm.1), custom_call_target="tpu_custom_call" | custom-call | tf_op jit(solution)/shard_map/pallas_call | solution.py:282
  69.7 1.9 %copy.8 = f32[128,1024]{1,0:T(8,128)} copy(f32[128,1024]{1,0:T(8,128)} %shard_map.46) | data formatting | bytes 1048576

commit v2 on v1

v2 whole, which is shorter than its diff:
```python
import functools

import jax
import jax.numpy as jnp
from jax import lax
from jax.experimental import pallas as pl
from jax.experimental.pallas import tpu as pltpu
from jax.sharding import PartitionSpec as P

LANES = 128
GROUP = 16
PEAK = 32000.0
CUTS = 1
LAG_PAIR, LAG_IN, LAG_CROSS, LAG_OUT, LAG_NEAR = 1, 1, 2, 2, 1
MESH = pl.DeviceIdType.MESH


def xor(a, b, size):
    both, bit = 0, 1
    while bit < size:
        both = both + bit * ((a // bit) % 2) * ((b // bit) % 2)
        bit *= 2
    return a + b - 2 * both


def encode(value, ref):
    rows, width = value.shape
    most = jnp.full((GROUP, LANES), 1e-30, jnp.float32)
    for at in range(width // LANES):
        part = jnp.abs(value[:, at * LANES:(at + 1) * LANES])
        most = jnp.maximum(most, jnp.max(part.reshape(rows // GROUP, GROUP, LANES), axis=0))
    power = jnp.ceil(jnp.log2(most))
    scale = jnp.tile(jnp.exp2(-power) * PEAK, (rows // GROUP, 1))
    for at in range(width // LANES):
        coded = jnp.round(value[:, at * LANES:(at + 1) * LANES] * scale)
        ref[at * rows:(at + 1) * rows, :] = coded.astype(jnp.int32).astype(jnp.int16)
    ref[rows * width // LANES:, :] = power.astype(jnp.int32).astype(jnp.int16)


def decode(ref, rows, width):
    power = ref[rows * width // LANES:, :].astype(jnp.int32).astype(jnp.float32)
    scale = jnp.tile(jnp.exp2(power) * (1.0 / PEAK), (rows // GROUP, 1))
    parts = [
        ref[at * rows:(at + 1) * rows, :].astype(jnp.int32).astype(jnp.float32) * scale
        for at in range(width // LANES)
    ]
    return jnp.concatenate(parts, axis=1)


def kernel(
    dims, cols_ref, counts_ref, v_hbm, f_hbm, out_ref,
    v_all, f_all, dense, own, pair_out, pair_in, held, chain_out, chain_in, cross_in, rowvals, part_out, part_in,
    load_sem, v_send, v_recv, pair_send, pair_recv, chain_send, chain_recv, cross_recv,
    far_send, far_recv, near_send, near_recv, part_send, part_recv,
):
    n_row, n_col, n_tiles, n_slots, tile, col_tiles, subs, cuts = dims
    n_pair = n_col // 2
    n_vec, width = out_ref.shape
    pieces, rows = n_row * subs, n_vec // subs
    half = n_tiles // 2 * tile
    thin = rows // cuts

    me_row, me_col = lax.axis_index("row"), lax.axis_index("col")
    pair, core = me_col // 2, me_col % 2
    partner = pair * 2 + 1 - core

    def last_pair(row):
        return jnp.minimum(n_pair - 1, ((row + 1) * n_tiles - 1) // (2 * col_tiles))

    last = last_pair(me_row)
    middle = last // 2
    left = pair <= middle
    active = pair <= last
    solo = last == 0
    center = jnp.logical_and(jnp.logical_or(pair == middle, pair == middle + 1), last > 0)
    depth = jnp.where(left, pair, last - pair)
    spread = jnp.where(left, middle - pair, pair - middle - 1)
    has_outer = depth > 0
    outer = jnp.where(left, pair - 1, pair + 1)
    inner = jnp.where(left, pair + 1, pair - 1)
    outer_col, inner_col = outer * 2 + core, inner * 2 + core
    in_lag = LAG_PAIR + LAG_IN * depth
    meet = LAG_PAIR + LAG_IN * jnp.maximum(middle, last - middle - 1) + LAG_CROSS
    total_lag = meet + LAG_OUT * spread
    final_lag = jnp.where(solo, LAG_PAIR, total_lag) + LAG_NEAR

    def peer_of(j):
        others = j - (subs - 1)
        is_last = j == pieces - 1 if subs > 1 else False
        is_own = jnp.logical_or(others < (1 if subs == 1 else 0), is_last)
        place = 0 if subs == 1 else jnp.where(is_last, subs - 1, j)
        shift = others - 1 if subs == 1 else others
        distance = jnp.where(is_own, 0, 1 + shift // subs)
        return distance, jnp.where(is_own, place, shift % subs), is_own

    def rows_of(place):
        return pl.ds(pl.multiple_of(place * rows, rows), rows)

    load_v = pltpu.make_async_copy(v_hbm, v_all.at[0], load_sem.at[0])
    load_f = pltpu.make_async_copy(f_hbm, f_all, load_sem.at[1])
    load_v.start()
    load_f.start()

    barrier = pltpu.get_barrier_semaphore()
    for k in range(1, n_row):
        pl.semaphore_signal(barrier, inc=1, device_id=(xor(me_row, k, n_row), me_col), device_id_type=MESH)
    pl.semaphore_signal(barrier, inc=1, device_id=(me_row, partner), device_id_type=MESH)

    @pl.when(pair > 0)
    def _():
        pl.semaphore_signal(barrier, inc=1, device_id=(me_row, me_col - 2), device_id_type=MESH)

    @pl.when(pair < n_pair - 1)
    def _():
        pl.semaphore_signal(barrier, inc=1, device_id=(me_row, me_col + 2), device_id_type=MESH)

    def remote(src, dst, send, recv, row, col):
        return pltpu.make_async_remote_copy(
            src_ref=src, dst_ref=dst, send_sem=send, recv_sem=recv, device_id=(row, col), device_id_type=MESH
        )

    def v_copy(k, place):
        return remote(
            v_hbm.at[rows_of(place)], v_all.at[k, rows_of(place)], v_send.at[k * subs + place],
            v_recv.at[k * subs + place], xor(me_row, k, n_row), me_col,
        )

    def pair_copy(j):
        return remote(pair_out.at[j], pair_in.at[j], pair_send.at[j], pair_recv.at[j], me_row, partner)

    def chain_copy(j, h):
        i = j * cuts + h
        return remote(chain_out.at[i], chain_in.at[i], chain_send.at[i], chain_recv.at[i], me_row, inner_col)

    def cross_copy(j, h):
        i = j * cuts + h
        return remote(chain_out.at[i], cross_in.at[i], chain_send.at[i], cross_recv.at[i], me_row, inner_col)

    def far_copy(j, h):
        i, ref = j * cuts + h, rowvals.at[core, j, h * thin:(h + 1) * thin]
        return remote(ref, ref, far_send.at[i], far_recv.at[i], me_row, outer_col)

    def near_copy(j, h):
        i, ref = j * cuts + h, rowvals.at[core, j, h * thin:(h + 1) * thin]
        return remote(ref, ref, near_send.at[i], near_recv.at[i], me_row, partner)

    def part_copy(j):
        return remote(
            part_out.at[j], part_in.at[j], part_send.at[j], part_recv.at[j], xor(me_row, peer_of(j)[0], n_row), me_col
        )

    load_f.wait()

    def build(start, stop):
        @pl.when(active)
        def _():
            @pl.loop(start, stop)
            def _(t):
                at = (t % (n_tiles // 2)) * tile
                count = jnp.broadcast_to(counts_ref[pl.ds(t, 1), :], (tile, tile))
                cols = [
                    jnp.where(s < count, jnp.broadcast_to(cols_ref[pl.ds(t, 1), s:s + 1], (tile, tile)), -1)
                    for s in range(n_slots)
                ]
                for c in range(col_tiles):
                    value = jnp.zeros((tile, tile), jnp.bfloat16)
                    for s in range(n_slots):
                        value = jnp.where(cols[s] == me_col * col_tiles + c, f_all[t, s], value)
                    dense[t // (n_tiles // 2), pl.ds(pl.multiple_of(at, tile), tile), c * tile:(c + 1) * tile] = value

    build(0, n_tiles // 2)

    edges = jnp.where(pair > 0, 1, 0) + jnp.where(pair < n_pair - 1, 1, 0)
    pl.semaphore_wait(barrier, n_row + edges)

    for k in range(1, n_row):
        @pl.when(pair <= last_pair(xor(me_row, k, n_row)))
        def _():
            for place in range(subs):
                v_copy(k, place).start()

    build(n_tiles // 2, n_tiles)
    load_v.wait()

    @pl.when(active)
    def _():
        @pl.loop(0, pieces + final_lag)
        def _(t):
            def valid(j):
                return jnp.logical_and(j >= 0, j < pieces)

            j_total = t - total_lag
            j_in = t - in_lag
            j_out = t - final_lag

            @pl.when(jnp.logical_and(valid(j_total), jnp.logical_not(solo)))
            def _():
                for h in range(cuts):
                    part_rows = slice(h * thin, (h + 1) * thin)

                    @pl.when(center)
                    def _():
                        cross_copy(j_total, h).wait_recv()
                        total = held[j_total, part_rows] + decode(cross_in.at[j_total * cuts + h], thin, half)
                        rowvals[core, j_total, part_rows] = total.astype(jnp.bfloat16)

                    @pl.when(jnp.logical_not(center))
                    def _():
                        far_copy(j_total, h).wait_recv()

                    @pl.when(has_outer)
                    def _():
                        far_copy(j_total, h).start()

                    near_copy(j_total, h).start()

            @pl.when(valid(j_in))
            def _():
                pair_copy(j_in).wait_recv()
                for h in range(cuts):
                    part_rows = slice(h * thin, (h + 1) * thin)
                    held[j_in, part_rows] = own[j_in, part_rows] + pair_in[j_in, part_rows]

                    @pl.when(has_outer)
                    def _():
                        chain_copy(j_in, h).wait_recv()
                        held[j_in, part_rows] += decode(chain_in.at[j_in * cuts + h], thin, half)

                    @pl.when(solo)
                    def _():
                        rowvals[core, j_in, part_rows] = held[j_in, part_rows].astype(jnp.bfloat16)
                        near_copy(j_in, h).start()

                    @pl.when(jnp.logical_not(solo))
                    def _():
                        encode(held[j_in, part_rows], chain_out.at[j_in * cuts + h])

                        @pl.when(center)
                        def _():
                            cross_copy(j_in, h).start()

                        @pl.when(jnp.logical_not(center))
                        def _():
                            chain_copy(j_in, h).start()

            @pl.when(t < pieces)
            def _():
                k, place, is_own = peer_of(t)

                @pl.when(jnp.logical_not(is_own))
                def _():
                    v_copy(k, place).wait_recv()

                vec = v_all[k, rows_of(place), :]
                dims_nt = (((1,), (1,)), ((), ()))
                pair_out[t] = lax.dot_general(vec, dense[1 - core], dims_nt, preferred_element_type=jnp.float32)
                pair_copy(t).start()
                own[t] = lax.dot_general(vec, dense[core], dims_nt, preferred_element_type=jnp.float32)

            @pl.when(valid(j_out))
            def _():
                for h in range(cuts):
                    near_copy(j_out, h).wait_recv()
                part = jnp.dot(rowvals[0, j_out], dense[0], preferred_element_type=jnp.float32)
                part += jnp.dot(rowvals[1, j_out], dense[1], preferred_element_type=jnp.float32)

                k, place, is_own = peer_of(j_out)

                @pl.when(is_own)
                def _():
                    out_ref[rows_of(place), :] = part

                @pl.when(jnp.logical_not(is_own))
                def _():
                    encode(part, part_out.at[j_out])
                    part_copy(j_out).start()

    @pl.when(jnp.logical_not(active))
    def _():
        out_ref[...] = jnp.zeros_like(out_ref)

    @pl.loop(0, pieces)
    def _(j):
        k, place, is_own = peer_of(j)

        @pl.when(jnp.logical_and(jnp.logical_not(is_own), pair <= last_pair(xor(me_row, k, n_row))))
        def _():
            part_copy(j).wait_recv()
            out_ref[rows_of(place), :] += decode(part_in.at[j], rows, width)

    for k in range(1, n_row):
        @pl.when(pair <= last_pair(xor(me_row, k, n_row)))
        def _():
            for place in range(subs):
                v_copy(k, place).wait_send()

    @pl.when(active)
    def _():
        @pl.loop(0, pieces)
        def _(j):
            pair_copy(j).wait_send()
            for h in range(cuts):
                near_copy(j, h).wait_send()

                @pl.when(jnp.logical_not(solo))
                def _():
                    chain_copy(j, h).wait_send()

                @pl.when(has_outer)
                def _():
                    far_copy(j, h).wait_send()

            @pl.when(jnp.logical_not(peer_of(j)[2]))
            def _():
                part_copy(j).wait_send()


def per_device(n_row, n_col, vectors, factor_tiles, tile_columns, live_counts):
    n_tiles, n_slots, tile, _ = factor_tiles.shape
    n_vec, width = vectors.shape
    subs = max(1, n_vec // 64)
    pieces, rows = n_row * subs, n_vec // subs
    half = n_tiles // 2 * tile
    cuts = max(1, min(CUTS, rows // GROUP))
    coded = rows // cuts * half // LANES + GROUP
    thin_pieces = pieces * cuts
    coded_out = rows * width // LANES + GROUP
    dma = pltpu.SemaphoreType.DMA
    return pl.pallas_call(
        functools.partial(kernel, (n_row, n_col, n_tiles, n_slots, tile, width // tile, subs, cuts)),
        out_shape=jax.ShapeDtypeStruct((n_vec, width), jnp.float32),
        in_specs=[
            pl.BlockSpec(memory_space=pltpu.VMEM),
            pl.BlockSpec(memory_space=pltpu.VMEM),
            pl.BlockSpec(memory_space=pl.ANY),
            pl.BlockSpec(memory_space=pl.ANY),
        ],
        out_specs=pl.BlockSpec(memory_space=pltpu.VMEM),
        scratch_shapes=[
            pltpu.VMEM((n_row, n_vec, width), jnp.bfloat16),
            pltpu.VMEM((n_tiles, n_slots, tile, tile), jnp.bfloat16),
            pltpu.VMEM((2, half, width), jnp.bfloat16),
            pltpu.VMEM((pieces, rows, half), jnp.float32),
            pltpu.VMEM((pieces, rows, half), jnp.float32),
            pltpu.VMEM((pieces, rows, half), jnp.float32),
            pltpu.VMEM((pieces, rows, half), jnp.float32),
            pltpu.VMEM((thin_pieces, coded, LANES), jnp.int16),
            pltpu.VMEM((thin_pieces, coded, LANES), jnp.int16),
            pltpu.VMEM((thin_pieces, coded, LANES), jnp.int16),
            pltpu.VMEM((2, pieces, rows, half), jnp.bfloat16),
            pltpu.VMEM((pieces, coded_out, LANES), jnp.int16),
            pltpu.VMEM((pieces, coded_out, LANES), jnp.int16),
            dma((2,)),
            dma((n_row * subs,)), dma((n_row * subs,)),
            dma((pieces,)), dma((pieces,)),
            dma((thin_pieces,)), dma((thin_pieces,)), dma((thin_pieces,)),
            dma((thin_pieces,)), dma((thin_pieces,)),
            dma((thin_pieces,)), dma((thin_pieces,)),
            dma((pieces,)), dma((pieces,)),
        ],
        compiler_params=pltpu.CompilerParams(
            collective_id=0, has_side_effects=True, vmem_limit_bytes=56 * 1024 * 1024
        ),
    )(tile_columns, live_counts, vectors, factor_tiles)


def solution(mesh):
    in_specs = (P("row", "col"), P("row", "col", None, None), P("row", "col"), P("row", "col"))
    out_specs = P("row", "col")
    body = functools.partial(per_device, mesh.shape["row"], mesh.shape["col"])
    return jax.shard_map(body, mesh=mesh, in_specs=in_specs, out_specs=out_specs, check_vma=False)
```

time: 71.8 us -> 59 us (0.82)
  Pallas kernels: 67 us -> 54.2 us
    pallas_call x1, Pallas kernels: 67 us -> 54.2 us  [per_device(): pl.pallas_call(functools.partial(kernel, (n_row, n_col, n_tiles, n_slots,...]
where the time goes in v2:
time: 59 us; the launch traced here: 58.8 us
  Pallas kernels  54.2 us (92%)
  local copies, waits for them, and re-layouts  4.55 us (8%)
    pallas_call x1, Pallas kernels, per_device(): pl.pallas_call(functools.partial(kernel, (n_row, n_col, n_tiles, n_slots,...  54.2 us
    unnamed x3, local copies, waits for them, and re-layouts  4.55 us

profile of v2, /device:TPU:0, one launch (start us, length us, event | category | flops | bytes accessed | tf_op | source)
XLA Modules:
  0.0 58.8 jit_solution(15447791539397077177)
XLA Ops:
  0.0 1.3 %copy.5.cols_ref = s32[8,3]{1,0:T(8,128)} copy(s32[8,3]{0,1:T(4,128)} %param.6) | data formatting | bytes 192 | tf_op args[2]
  1.3 1.3 %copy.6.counts_ref = s32[8,1]{1,0:T(8,128)} copy(s32[8,1]{0,1:T(1,128)} %param.7) | data formatting | bytes 64 | tf_op args[3]
  2.7 54.2 %shard_map.46 = f32[128,1024]{1,0:T(8,128)} custom-call(s32[8,3]{1,0:T(8,128)} %copy.5.cols_ref, s32[8,1]{1,0:T(8,128)} %copy.6.counts_ref, bf16[128,1024]{1,0:T(8,128)(2,1)} %v_hbm.1, bf16[8,3,256,256]{3,2,1,0:T(8,128)(2,1)} %f_hbm.1), custom_call_target="tpu_custom_call" | custom-call | tf_op jit(solution)/shard_map/pallas_call | solution.py:329
  56.9 1.9 %copy.8 = f32[128,1024]{1,0:T(8,128)} copy(f32[128,1024]{1,0:T(8,128)} %shard_map.46) | data formatting | bytes 1048576

commit v3 on v2

--- a/solution.py
+++ b/solution.py
@@ -11,7 +11,7 @@
 GROUP = 16
 PEAK = 32000.0
 CUTS = 1
-LAG_PAIR, LAG_IN, LAG_CROSS, LAG_OUT, LAG_NEAR = 1, 1, 2, 2, 1
+LAG_PAIR, LAG_IN, LAG_CROSS, LAG_OUT, LAG_NEAR = 1, 2, 2, 2, 1
 MESH = pl.DeviceIdType.MESH
 
 
@@ -48,7 +48,7 @@
 
 
 def kernel(
-    dims, cols_ref, counts_ref, v_hbm, f_hbm, out_ref,
+    dims, cols_ref, v_hbm, f_hbm, out_ref,
     v_all, f_all, dense, own, pair_out, pair_in, held, chain_out, chain_in, cross_in, rowvals, part_out, part_in,
     load_sem, v_send, v_recv, pair_send, pair_recv, chain_send, chain_recv, cross_recv,
     far_send, far_recv, near_send, near_recv, part_send, part_recv,
@@ -157,15 +157,14 @@
             @pl.loop(start, stop)
             def _(t):
                 at = (t % (n_tiles // 2)) * tile
-                count = jnp.broadcast_to(counts_ref[pl.ds(t, 1), :], (tile, tile))
                 cols = [
-                    jnp.where(s < count, jnp.broadcast_to(cols_ref[pl.ds(t, 1), s:s + 1], (tile, tile)), -1)
+                    jnp.broadcast_to(cols_ref[pl.ds(t, 1), s:s + 1], (tile, tile))
                     for s in range(n_slots)
                 ]
                 for c in range(col_tiles):
                     value = jnp.zeros((tile, tile), jnp.bfloat16)
                     for s in range(n_slots):
-                        value = jnp.where(cols[s] == me_col * col_tiles + c, f_all[t, s], value)
+                        value = jnp.where(cols[s] == c, f_all[t, s], value)
                     dense[t // (n_tiles // 2), pl.ds(pl.multiple_of(at, tile), tile), c * tile:(c + 1) * tile] = value
 
     build(0, n_tiles // 2)
@@ -326,11 +325,12 @@
     thin_pieces = pieces * cuts
     coded_out = rows * width // LANES + GROUP
     dma = pltpu.SemaphoreType.DMA
+    slot = lax.broadcasted_iota(jnp.int32, tile_columns.shape, 1)
+    places = jnp.where(slot < live_counts, tile_columns - lax.axis_index("col") * (width // tile), -1)
     return pl.pallas_call(
         functools.partial(kernel, (n_row, n_col, n_tiles, n_slots, tile, width // tile, subs, cuts)),
         out_shape=jax.ShapeDtypeStruct((n_vec, width), jnp.float32),
         in_specs=[
-            pl.BlockSpec(memory_space=pltpu.VMEM),
             pl.BlockSpec(memory_space=pltpu.VMEM),
             pl.BlockSpec(memory_space=pl.ANY),
             pl.BlockSpec(memory_space=pl.ANY),
@@ -361,7 +361,7 @@
         compiler_params=pltpu.CompilerParams(
             collective_id=0, has_side_effects=True, vmem_limit_bytes=56 * 1024 * 1024
         ),
-    )(tile_columns, live_counts, vectors, factor_tiles)
+    )(places, vectors, factor_tiles)
 
 
 def solution(mesh):

time: 59 us -> 57.9 us (0.981)
  local copies, waits for them, and re-layouts: 4.55 us -> 2.64 us
  other arithmetic: 0 us -> 1.32 us
    unnamed x3 -> x2, local copies, waits for them, and re-layouts: 4.55 us -> 2.64 us
    select_n x0 -> x1, other arithmetic: none -> 1.32 us  [per_device(): jnp.where(slot < live_counts, tile_columns - lax.axis_index('col') * (wid...]
where the time goes in v3:
time: 57.9 us; the launch traced here: 57.6 us
  Pallas kernels  53.7 us (93%)
  local copies, waits for them, and re-layouts  2.64 us (5%)
  other arithmetic  1.32 us (2%)
    pallas_call x1, Pallas kernels, per_device(): pl.pallas_call(functools.partial(kernel, (n_row, n_col, n_tiles, n_slots,...  53.7 us
    unnamed x2, local copies, waits for them, and re-layouts  2.64 us
    select_n x1, other arithmetic, per_device(): jnp.where(slot < live_counts, tile_columns - lax.axis_index('col') * (wid...  1.32 us

profile of v3, /device:TPU:0, one launch (start us, length us, event | category | flops | bytes accessed | tf_op | source)
XLA Modules:
  0.0 57.6 jit_solution(8759582397151860109)
XLA Ops:
  0.0 0.8 %copy.5 = s32[8,3]{1,0:T(8,128)S(1)} copy(s32[8,3]{0,1:T(4,128)} %param.6) | data formatting | bytes 192 | tf_op args[2]
  0.8 1.3 %subtract_select_fusion.cols_ref = s32[8,3]{1,0:T(8,128)} fusion(s32[8,3]{1,0:T(8,128)S(1)} %copy.5, s32[]{:T(128)S(6)} %mul.3, s32[8]{0:T(128)} %bitcast.1), kind=kLoop, calls=%fused_computation | loop fusion | flops 72 | bytes 228 | tf_op jit(solution)/shard_map/jit(_where)/select_n | solution.py:329
  2.1 53.7 %shard_map.46 = f32[128,1024]{1,0:T(8,128)} custom-call(s32[8,3]{1,0:T(8,128)} %subtract_select_fusion.cols_ref, bf16[128,1024]{1,0:T(8,128)(2,1)} %v_hbm.1, bf16[8,3,256,256]{3,2,1,0:T(8,128)(2,1)} %f_hbm.1), custom_call_target="tpu_custom_call" | custom-call | tf_op jit(solution)/shard_map/pallas_call | solution.py:330
  55.7 1.9 %copy.7 = f32[128,1024]{1,0:T(8,128)} copy(f32[128,1024]{1,0:T(8,128)} %shard_map.46) | data formatting | bytes 1048576
